TPU v7x, 32 devices: a whole 2x2x4 slice. The times are simulated.
32 devices in a mesh: ens: 16 (over z, y, x), slab: 2 (over core).
Axes of the slice: x: 2, y: 2, z: 4, core: 2. Of those that a mesh axis runs over, the one named last changes fastest.
Arguments:
- ensemble: float32 [16, 3, 128, 768], P('ens', None, 'slab'), may hold values from -6 to 6
- perturbation: float32 [16, 3, 128, 768], P('ens', None, 'slab'), may hold values from -6 to 6
- ancestors: int32 [16], P('ens'), may hold values from 0 to 15
- bathymetry: int32 [128, 768], replicated, may hold values from 50 to 200
Outputs:
- analysis: float32 [16, 3, 128, 768], P('ens', None, 'slab')
Inputs may be any that keep to these rules, and one draw needn't show every extreme that they name: `ancestors`: each entry names the old particle that a new particle copies.
All inputs are finite; a program needn't handle non-finite values.
Results may differ from a plain program's by a relative error of at most 0.00002.
Values sent between devices are 32-bit elements; how exact they have to be, the bound alone decides.
A program may use at most 128 MiB of HBM per device.

v0:
```python
import jax
import jax.numpy as jnp
from jax import lax
from jax.sharding import PartitionSpec as P

STEPS = 3


RATIO = 0.3
TURNING = 0.03
JITTER = 0.5


def padded(cells, sides, width):
    for axis, dim in sides:
        count = lax.axis_size(axis)
        ends = count - 1
        head = lax.slice_in_dim(cells, 0, width, axis=dim)
        tail = lax.slice_in_dim(cells, cells.shape[dim] - width, cells.shape[dim], axis=dim)
        cells = jnp.concatenate(
            [
                lax.ppermute(tail, axis, [(i, (i + 1) % count) for i in range(ends)]),
                cells,
                lax.ppermute(head, axis, [((i + 1) % count, i) for i in range(ends)]),
            ],
            axis=dim,
        )
    return cells


def eastward_difference(field):
    return (jnp.roll(field, -1, -1) - jnp.roll(field, 1, -1)) * 0.5


def step_rows(height, east_vel, north_vel, ocean_floor, inside):
    flux_east = ocean_floor * east_vel
    flux_north = ocean_floor * north_vel
    height_next = height[1:-1] - RATIO * (
        eastward_difference(flux_east[1:-1]) + (flux_north[2:] - flux_north[:-2]) * 0.5
    )
    height_next = jnp.where(inside[1:-1], height_next, 0.0)
    east_next = (
        east_vel[2:-2] - RATIO * eastward_difference(height_next[1:-1]) + TURNING * north_vel[2:-2]
    )
    north_next = (
        north_vel[2:-2]
        - RATIO * (height_next[2:] - height_next[:-2]) * 0.5
        - TURNING * east_vel[2:-2]
    )
    kept = inside[2:-2]
    return (height_next[1:-1], jnp.where(kept, east_next, 0.0), jnp.where(kept, north_next, 0.0))


def edge_rows(members, depth):
    return jnp.stack(
        [jnp.concatenate([member[:depth], member[-depth:]], axis=0) for member in members]
    )


def attach_rims(members, rims, depth):
    return [
        jnp.concatenate([rims[k, :depth], members[k], rims[k, 3 * depth :]], axis=0)
        for k in range(len(members))
    ]


def pick_rows(portion, lineage):
    return jnp.take(portion, lineage, axis=0, mode="clip")


def shards(ensemble, perturbation, ancestors, bathymetry):
    row_count = ensemble.shape[2]
    col_count = ensemble.shape[3]
    total_rows = bathymetry.shape[0]
    first_row = lax.axis_index("slab") * row_count
    widest = 2 * STEPS
    seabed_all = jnp.pad(bathymetry.astype(jnp.float32) * 0.01, ((widest, widest), (0, 0)))
    members = [ensemble[0, 0], ensemble[0, 1], ensemble[0, 2]]
    ocean_floor = lax.dynamic_slice_in_dim(seabed_all, first_row + widest - 2, row_count + 2 * 2, 0)
    global_row = first_row - 2 + jnp.arange(row_count + 2 * 2, dtype=jnp.int32)
    inside = ((global_row >= 0) & (global_row < total_rows))[:, None]
    ocean_floor, inside = (ocean_floor, inside)
    for substep in range(STEPS):
        rims = padded(edge_rows(members, 2), (("slab", 1),), 2)
        widened = attach_rims(members, rims, 2)
        members = list(step_rows(widened[0], widened[1], widened[2], ocean_floor, inside))
    noise = [perturbation[0, 0], perturbation[0, 1], perturbation[0, 2]]
    noise_rims = padded(edge_rows(noise, 1), (("slab", 1),), 1)
    bordered = attach_rims(noise, noise_rims, 1)
    smoothed = jnp.stack(
        [
            (
                4.0 * cell[1:-1]
                + cell[2:]
                + cell[:-2]
                + jnp.roll(cell[1:-1], 1, -1)
                + jnp.roll(cell[1:-1], -1, -1)
            )
            * 0.125
            for cell in bordered
        ]
    )
    lineage = lax.all_gather(ancestors, "ens", axis=0, tiled=True)
    flattened = jnp.stack(members).reshape(1, 3, row_count * col_count)
    pieces = lax.all_to_all(flattened, "ens", split_axis=2, concat_axis=0, tiled=True)
    picked = pick_rows(pieces, lineage)
    returned = lax.all_to_all(picked, "ens", split_axis=0, concat_axis=2, tiled=True)
    selected_parents = returned.reshape(1, 3, row_count, col_count)
    return selected_parents + JITTER * smoothed[None]


def solution(mesh):
    in_specs = (P("ens", None, "slab", None), P("ens", None, "slab", None), P("ens"), P())
    out_specs = P("ens", None, "slab", None)
    return jax.shard_map(shards, mesh=mesh, in_specs=in_specs, out_specs=out_specs, check_vma=False)
```

profile of v0, /device:TPU:0, one launch (start us, length us, event | category | flops | bytes accessed | tf_op | source)
XLA Modules:
  0.0 422.1 jit_solution(13704368360350379252)
XLA Ops:
  0.0 0.8 slice_bitcast_fusion.29
  0.9 2.4 collective-permute-start
  3.3 1.3 collective-permute-start.1
  4.6 1.2 slice_bitcast_fusion.4
  5.8 1.0 convert_multiply_fusion
  6.8 0.8 slice_bitcast_fusion.41
  7.7 0.1 slice.474
  7.8 0.1 slice.507
  7.9 0.1 maximum_multiply_fusion.1
  8.0 0.1 fusion.68
  8.1 0.1 fusion.67
  8.2 0.2 fusion.12
  8.4 0.1 fusion.66
  8.5 0.1 fusion.65
  8.6 1.2 fusion.46
  9.9 3.0 collective-permute-start.2
  13.0 1.3 collective-permute-start.3
  14.3 1.8 collective-permute-done.3
  16.1 0.1 maximum_multiply_fusion.3
  16.1 0.1 fusion.63
  16.3 0.1 fusion.62
  16.3 0.2 fusion.8
  16.5 0.1 fusion.61
  16.7 0.1 fusion.60
  16.7 0.2 fusion.50
  17.0 2.1 collective-permute-start.4
  19.1 1.3 collective-permute-start.6
  20.4 3.0 collective-permute-start.7
  23.5 1.5 collective-permute-start.5
  25.0 1.6 collective-permute-done.5
  26.5 0.1 maximum_multiply_fusion.5
  26.6 0.1 fusion.58
  26.7 0.1 fusion.57
  26.8 0.2 fusion.4
  27.0 0.1 fusion.56
  27.1 0.1 fusion.55
  27.2 0.2 fusion.54
  27.3 0.2 stack.84
  27.6 0.2 stack.85
  27.8 0.2 stack.86
  28.0 0.5 pad_maximum_fusion
  28.5 35.5 %copy.21 = f32[1,3,49152]{1,0,2:T(1,128)} copy(f32[1,3,49152]{2,1,0:T(4,128)S(1)} %pad_maximum_fusion) | data formatting | bytes 1179648 | tf_op jit(solution)/shard_map/stack | solution.py:104
  64.0 0.5 broadcast.54
  64.6 218.6 %reduce = f32[49152,3]{1,0:T(8,128)} reduce(f32[49152,1,3]{2,1,0:T(1,128)} %bitcast.134, f32[]{:T(128)} %broadcast.54), dimensions={1}, to_apply=%bitcast.132.reduce_sub_computation | reduce | bytes 1179652
  283.2 22.2 %reshape.100 = f32[16,1,9216]{2,1,0:T(1,128)} reshape(f32[49152,3]{1,0:T(8,128)} %reduce) | data formatting | bytes 1179648
  305.4 7.7 %all-to-all-start = ((f32[16,1,9216]{2,1,0:T(1,128)}), f32[16,1,9216]{2,1,0:T(1,128)S(1)}, u32[]{:S(2)}, u32[]{:S(2)}) async-start(f32[16,1,9216]{2,1,0:T(1,128)} %reshape.100), calls=%async_computation | async-start | bytes 1179648 | tf_op jit(solution)/shard_map/all_to_all | solution.py:105
  313.8 0.6 dynamic-slice
  314.4 0.7 dynamic-update-slice
  315.1 14.8 %all-reduce.1 = s32[16]{0:T(128)S(1)} all-reduce(s32[16]{0:T(128)S(1)} %dynamic-update-slice), channel_id=1, replica_groups=mesh['ens'=16,'slab'=2] {'ens'}, use_global_device_ids=true, to_apply=%add.1 | all-reduce | flops 16 | bytes 128
  330.1 0.1 fusion.70
  330.1 0.1 fusion.73
  330.3 0.2 fusion.69
  330.5 2.0 reduce.1
  332.5 48.9 %reshape.101 = f32[49152,1,3]{2,1,0:T(1,128)} reshape(f32[16,9216]{1,0:T(8,128)S(1)} %reduce.1) | data formatting | bytes 1179648
  381.4 14.0 %copy.23 = f32[1,3,16,3072]{3,1,2,0:T(4,128)S(1)} copy(f32[1,3,16,3072]{1,3,2,0:T(8,128)} %bitcast.135) | data formatting | bytes 1179648 | tf_op jit(solution)/shard_map/all_to_all | solution.py:105
  395.4 1.9 gather_fusion
  397.2 4.0 all-to-all-start.1
  401.3 0.1 fusion.23
  401.4 0.1 fusion.29
  401.6 0.1 fusion.17
  401.7 19.0 %all-to-all-done.1 = f32[16,3,3072]{2,1,0:T(4,128)S(1)} async-done(((f32[16,3,3072]{2,1,0:T(4,128)}), f32[16,3,3072]{2,1,0:T(4,128)S(1)}, u32[]{:S(2)}, u32[]{:S(2)}) %all-to-all-start.1) | async-done | bytes 589856 | tf_op jit(solution)/shard_map/all_to_all | solution.py:107
  420.7 0.3 copy.24
  421.0 0.2 reshape.85
  421.2 0.9 fusion
  (48 shorter events, 0.5 us)
Async XLA Ops:
  0.9 7.0 %collective-permute-start = (f32[3,2,768]{2,1,0:T(2,128)S(1)}, f32[3,2,768]{2,1,0:T(2,128)S(1)}, u32[]{:S(2)}, u32[]{:S(2)}) collective-permute-start(f32[3,2,768]{2,1,0:T(2,128)S(1)} %get-tuple-element.90), channel_id=1, source_target_pairs={{0,1},{2,3},{4,5},{6,7},{8,9},{10,11},{12,13},{14,15},{16,17},{18,... | collective-permute-start | bytes 55304 | tf_op jit(solution)/shard_map/ppermute | solution.py:22
  3.3 4.6 %collective-permute-start.1 = (f32[3,2,768]{2,1,0:T(2,128)S(1)}, f32[3,2,768]{2,1,0:T(2,128)S(1)}, u32[]{:S(2)}, u32[]{:S(2)}) collective-permute-start(f32[3,2,768]{2,1,0:T(2,128)S(1)} %get-tuple-element.91), channel_id=1, source_target_pairs={{1,0},{3,2},{5,4},{7,6},{9,8},{11,10},{13,12},{15,14},{17,16},{19,... | collective-permute-start | bytes 55304 | tf_op jit(solution)/shard_map/ppermute | solution.py:24
  9.9 4.4 %collective-permute-start.2 = (f32[3,2,768]{2,1,0:T(2,128)S(1)}, f32[3,2,768]{2,1,0:T(2,128)S(1)}, u32[]{:S(2)}, u32[]{:S(2)}) collective-permute-start(f32[3,2,768]{2,1,0:T(2,128)S(1)} %get-tuple-element.88), channel_id=1, source_target_pairs={{0,1},{2,3},{4,5},{6,7},{8,9},{10,11},{12,13},{14,15},{16,17},{18,... | collective-permute-start | bytes 55304 | tf_op jit(solution)/shard_map/ppermute | solution.py:22
  13.0 3.1 collective-permute-start.3
  17.0 7.9 %collective-permute-start.4 = (f32[3,2,768]{2,1,0:T(2,128)S(1)}, f32[3,2,768]{2,1,0:T(2,128)S(1)}, u32[]{:S(2)}, u32[]{:S(2)}) collective-permute-start(f32[3,2,768]{2,1,0:T(2,128)S(1)} %get-tuple-element.86), channel_id=1, source_target_pairs={{0,1},{2,3},{4,5},{6,7},{8,9},{10,11},{12,13},{14,15},{16,17},{18,... | collective-permute-start | bytes 55304 | tf_op jit(solution)/shard_map/ppermute | solution.py:22
  19.1 382.1 %collective-permute-start.6 = (f32[3,1,768]{2,1,0:T(1,128)S(1)}, f32[3,1,768]{2,1,0:T(1,128)S(1)}, u32[]{:S(2)}, u32[]{:S(2)}) collective-permute-start(f32[3,1,768]{2,1,0:T(1,128)S(1)} %get-tuple-element.92), channel_id=1, source_target_pairs={{1,0},{3,2},{5,4},{7,6},{9,8},{11,10},{13,12},{15,14},{17,16},{19,... | collective-permute-start | bytes 27656 | tf_op jit(solution)/shard_map/ppermute | solution.py:24
  20.4 380.9 %collective-permute-start.7 = (f32[3,1,768]{2,1,0:T(1,128)S(1)}, f32[3,1,768]{2,1,0:T(1,128)S(1)}, u32[]{:S(2)}, u32[]{:S(2)}) collective-permute-start(f32[3,1,768]{2,1,0:T(1,128)S(1)} %get-tuple-element.93), channel_id=1, source_target_pairs={{0,1},{2,3},{4,5},{6,7},{8,9},{10,11},{12,13},{14,15},{16,17},{18,... | collective-permute-start | bytes 27656 | tf_op jit(solution)/shard_map/ppermute | solution.py:22
  23.5 3.1 collective-permute-start.5
  283.2 29.9 %copy-start = (f32[1,3,64,768]{3,2,1,0:T(8,128)S(1)}, f32[1,3,64,768]{3,2,1,0:T(8,128)}, u32[]{:S(2)}) copy-start(f32[1,3,64,768]{3,2,1,0:T(8,128)} %param.5) | copy-start | bytes 1769476
  283.2 30.6 %copy-start.1 = (u32[32]{0:T(128)S(1)}, u32[32]{0:T(128)}, u32[]{:S(2)}) copy-start(u32[32]{0:T(128)} %constant.55) | copy-start | bytes 388
  305.4 25.1 %all-to-all-start = ((f32[16,1,9216]{2,1,0:T(1,128)}), f32[16,1,9216]{2,1,0:T(1,128)S(1)}, u32[]{:S(2)}, u32[]{:S(2)}) async-start(f32[16,1,9216]{2,1,0:T(1,128)} %reshape.100), calls=%async_computation | async-start | bytes 1179648 | tf_op jit(solution)/shard_map/all_to_all | solution.py:105
  397.2 23.5 %all-to-all-start.1 = ((f32[16,3,3072]{2,1,0:T(4,128)}), f32[16,3,3072]{2,1,0:T(4,128)S(1)}, u32[]{:S(2)}, u32[]{:S(2)}) async-start(f32[16,3,3072]{2,1,0:T(4,128)} %gather_fusion), calls=%async_computation.1 | async-start | bytes 1572864 | tf_op jit(solution)/shard_map/all_to_all | solution.py:107
where the time goes:
time: 423 us; the launch traced here: 422 us
  other arithmetic  226 us (53%)
  local copies, waits for them, and re-layouts  130 us (31%)
  starting transfers between devices  27.6 us (7%)
  waiting for transfers between devices  22.3 us (5%)
  blocking collectives  14.8 us (3%)
    unnamed x1, other arithmetic  219 us
    unnamed x10, local copies, waits for them, and re-layouts  73 us
    another operation x4, local copies, waits for them, and re-layouts, shards(): flattened = jnp.stack(members).reshape(1, 3, row_count * col_count)  36.1 us
    all_to_all x1, waiting for transfers between devices, shards(): lax.all_to_all(picked, 'ens', split_axis=0, concat_axis=2, tiled=True)  19 us
    unnamed x1, blocking collectives  14.8 us
    all_to_all x1, local copies, waits for them, and re-layouts, shards(): lax.all_to_all(flattened, 'ens', split_axis=2, concat_axis=0, tiled=True)  14 us
    ppermute x4, starting transfers between devices, padded(): lax.ppermute(tail, axis, [(i, (i + 1) % count) for i in range(ends)])  10.5 us
  transfers between devices with their start and end apart: 10, of which 3 were waited for; matrix products, arithmetic and copies ran while one was open for 83% of the time, Pallas kernels for 0%

commit v1 on v0

--- a/solution.py
+++ b/solution.py
@@ -1,9 +1,16 @@
+import functools
+
 import jax
 import jax.numpy as jnp
 from jax import lax
+from jax.experimental import pallas as pl
+from jax.experimental.pallas import tpu as pltpu
 from jax.sharding import PartitionSpec as P
 
 STEPS = 3
+MESH = pl.DeviceIdType.MESH
+STRIP = 8
+LANES = 128
 
 
 RATIO = 0.3
@@ -109,7 +116,237 @@
     return selected_parents + JITTER * smoothed[None]
 
 
+def whole_wait(ref, sem):
+    pltpu.make_async_copy(ref, ref, sem).wait()
+
+
+def cycle_kernel(
+    n, rows, cols, across,
+    ens_ref, pert_ref, anc_ref, bath_ref, out_ref,
+    state, noise, sb, pieces0, pieces1, pieces2, picked, res, lin_v, lin_s,
+    halo_send, halo_recv, lin_send, lin_recv, lin_local,
+    a_send, a_recv, b_send, b_recv,
+):
+    me = lax.axis_index("ens")
+    s = lax.axis_index("slab")
+    width = cols // across
+    pieces = (pieces0, pieces1, pieces2)
+    top = STRIP
+    bottom = STRIP + rows
+    barrier = pltpu.get_barrier_semaphore()
+
+    def peer(t):
+        offset = n // 2 + (1 - 2 * (t % 2)) * ((t + 1) // 2)
+        return lax.rem(me + offset, n)
+
+    def each_peer(body):
+        def run(t, carry):
+            body(t, peer(t))
+            return carry
+
+        lax.fori_loop(0, n - 1, run, 0)
+
+    def greet(t, to):
+        pl.semaphore_signal(barrier, inc=1, device_id={"ens": to}, device_id_type=MESH)
+
+    each_peer(greet)
+    pl.semaphore_signal(barrier, inc=1, device_id={"slab": 1 - s}, device_id_type=MESH)
+
+    lin_v[me] = jnp.full((1, LANES), anc_ref[0], jnp.int32)
+    wall = pl.multiple_of(s * (rows + STRIP), STRIP)
+    open_side = pl.multiple_of((1 - s) * (rows + STRIP), STRIP)
+    zeros = jnp.zeros((STRIP, cols), jnp.float32)
+    for f in range(3):
+        state[f, pl.ds(wall, STRIP)] = zeros
+        noise[f, pl.ds(wall, STRIP)] = zeros
+        for r in range(0, rows, STRIP):
+            state[f, top + r : top + r + STRIP] = ens_ref[f, r : r + STRIP]
+            noise[f, top + r : top + r + STRIP] = pert_ref[f, r : r + STRIP]
+    sb[pl.ds(wall, STRIP)] = zeros
+    beyond = pl.multiple_of(rows - STRIP * s, STRIP)
+    sb[pl.ds(open_side, STRIP)] = bath_ref[pl.ds(beyond, STRIP)].astype(jnp.float32) * 0.01
+    first = pl.multiple_of(s * rows, STRIP)
+    for r in range(0, rows, STRIP):
+        sb[top + r : top + r + STRIP] = (
+            bath_ref[pl.ds(pl.multiple_of(first + r, STRIP), STRIP)].astype(jnp.float32) * 0.01
+        )
+
+    pl.semaphore_wait(barrier, n)
+
+    edge = pl.multiple_of((1 - s) * (rows - STRIP), STRIP)
+    halos = []
+    for i, (src, dst) in enumerate(((ens_ref, state), (pert_ref, noise))):
+        copy = pltpu.make_async_remote_copy(
+            src_ref=src.at[:, pl.ds(edge, STRIP)],
+            dst_ref=dst.at[:, pl.ds(wall, STRIP)],
+            send_sem=halo_send.at[i],
+            recv_sem=halo_recv.at[i],
+            device_id={"slab": 1 - s},
+            device_id_type=MESH,
+        )
+        copy.start()
+        halos.append(copy)
+
+    def tell(t, to):
+        pltpu.make_async_remote_copy(
+            src_ref=lin_v.at[me],
+            dst_ref=lin_v.at[me],
+            send_sem=lin_send,
+            recv_sem=lin_recv,
+            device_id={"ens": to},
+            device_id_type=MESH,
+        ).start()
+
+    each_peer(tell)
+    halos[0].wait()
+
+    def shifted(f, r, by):
+        source = sb if f is None else state.at[f]
+        if 0 <= r + by <= rows + STRIP:
+            return source[r + by : r + by + STRIP]
+        return pltpu.roll(source[r : r + STRIP], -by % STRIP, 0)
+
+    def east(x):
+        return (pltpu.roll(x, cols - 1, 1) - pltpu.roll(x, 1, 1)) * 0.5
+
+    def heights(r):
+        here = slice(r, r + STRIP)
+        northward = shifted(None, r, 1) * shifted(2, r, 1) - shifted(None, r, -1) * shifted(2, r, -1)
+        new = state[0, here] - RATIO * (east(sb[here] * state[1, here]) + northward * 0.5)
+        if r == 0:
+            new = jnp.where(s == 1, new, 0.0)
+        if r == bottom:
+            new = jnp.where(s == 0, new, 0.0)
+        state[0, here] = new
+
+    def velocities(r):
+        here = slice(r, r + STRIP)
+        u = state[1, here]
+        v = state[2, here]
+        state[1, here] = u - RATIO * east(state[0, here]) + TURNING * v
+        northward = (shifted(0, r, 1) - shifted(0, r, -1)) * 0.5
+        state[2, here] = v - RATIO * northward - TURNING * u
+
+    def spot(ref, f, index, base):
+        r = pl.multiple_of(base + (index // across) * STRIP, STRIP)
+        c = pl.multiple_of((index % across) * width, LANES)
+        return ref.at[f, pl.ds(r, STRIP), pl.ds(c, width)]
+
+    def scatter(f):
+        def send(t, to):
+            pltpu.make_async_remote_copy(
+                src_ref=spot(state, f, to, top),
+                dst_ref=pieces[f].at[me],
+                send_sem=a_send.at[f],
+                recv_sem=a_recv.at[f],
+                device_id={"ens": to},
+                device_id_type=MESH,
+            ).start()
+
+        each_peer(send)
+        pltpu.make_async_copy(spot(state, f, me, top), pieces[f].at[me], a_recv.at[f]).start()
+
+    for step in range(STEPS):
+        last = step == STEPS - 1
+        for r in range(0, bottom + STRIP, STRIP):
+            heights(r)
+        if last:
+            scatter(0)
+        for r in range(top if last else 0, bottom if last else bottom + STRIP, STRIP):
+            velocities(r)
+    scatter(1)
+    scatter(2)
+
+    halos[1].wait()
+    for f in range(3):
+        for r in range(top, bottom, STRIP):
+            p = noise[f, r : r + STRIP]
+            around = noise[f, r + 1 : r + 1 + STRIP] + noise[f, r - 1 : r - 1 + STRIP]
+            total = 4.0 * p + around + pltpu.roll(p, 1, 1) + pltpu.roll(p, cols - 1, 1)
+            out_ref[f, r - top : r - top + STRIP] = total * 0.125 * JITTER
+
+    whole_wait(lin_v.at[pl.ds(0, n - 1)], lin_recv)
+    fetch = pltpu.make_async_copy(lin_v, lin_s, lin_local)
+    fetch.start()
+    fetch.wait()
+
+    for f in range(3):
+        whole_wait(pieces[f], a_recv.at[f])
+
+        def reply(t, to):
+            picked[f, t] = pieces[f][lin_s[to, 0, 0]]
+            pltpu.make_async_remote_copy(
+                src_ref=picked.at[f, t],
+                dst_ref=spot(res, f, me, 0),
+                send_sem=b_send.at[f],
+                recv_sem=b_recv.at[f],
+                device_id={"ens": to},
+                device_id_type=MESH,
+            ).start()
+
+        each_peer(reply)
+        picked[f, n - 1] = pieces[f][lin_s[me, 0, 0]]
+        pltpu.make_async_copy(picked.at[f, n - 1], spot(res, f, me, 0), b_recv.at[f]).start()
+
+    for f in range(3):
+        whole_wait(res.at[f], b_recv.at[f])
+        for r in range(0, rows, STRIP):
+            out_ref[f, r : r + STRIP] = res[f, r : r + STRIP] + out_ref[f, r : r + STRIP]
+    whole_wait(lin_v.at[pl.ds(0, n - 1)], lin_send)
+    for f in range(3):
+        whole_wait(pieces[f].at[pl.ds(0, n - 1)], a_send.at[f])
+        whole_wait(picked.at[f, pl.ds(0, n - 1)], b_send.at[f])
+
+
+def cycle(n, ensemble, perturbation, ancestors, bathymetry):
+    rows, cols = ensemble.shape[2:]
+    across = n * STRIP // rows
+    tall = rows + 2 * STRIP
+    f32 = jnp.float32
+    vmem = pl.BlockSpec(memory_space=pltpu.VMEM)
+    dma = pltpu.SemaphoreType.DMA
+    result = pl.pallas_call(
+        functools.partial(cycle_kernel, n, rows, cols, across),
+        out_shape=jax.ShapeDtypeStruct((3, rows, cols), f32),
+        in_specs=[vmem, vmem, pl.BlockSpec(memory_space=pltpu.SMEM), vmem],
+        out_specs=vmem,
+        scratch_shapes=[
+            pltpu.VMEM((3, tall, cols), f32),
+            pltpu.VMEM((3, tall, cols), f32),
+            pltpu.VMEM((tall, cols), f32),
+            pltpu.VMEM((n, STRIP, cols // across), f32),
+            pltpu.VMEM((n, STRIP, cols // across), f32),
+            pltpu.VMEM((n, STRIP, cols // across), f32),
+            pltpu.VMEM((3, n, STRIP, cols // across), f32),
+            pltpu.VMEM((3, rows, cols), f32),
+            pltpu.VMEM((n, 1, LANES), jnp.int32),
+            pltpu.SMEM((n, 1, LANES), jnp.int32),
+            dma((2,)), dma((2,)), dma(()), dma(()), dma(()),
+            dma((3,)), dma((3,)), dma((3,)), dma((3,)),
+        ],
+        compiler_params=pltpu.CompilerParams(collective_id=0, has_side_effects=True),
+        name="cycle",
+    )(ensemble[0], perturbation[0], ancestors, bathymetry)
+    return result[None]
+
+
+def fits(mesh, ensemble):
+    n, slabs = mesh.shape["ens"], mesh.shape["slab"]
+    rows, cols = ensemble.shape[2] // slabs, ensemble.shape[3]
+    strips = rows // STRIP
+    if slabs != 2 or ensemble.shape[0] != n or rows % STRIP or n % strips:
+        return False
+    across = n // strips
+    return cols % (across * LANES) == 0
+
+
 def solution(mesh):
     in_specs = (P("ens", None, "slab", None), P("ens", None, "slab", None), P("ens"), P())
     out_specs = P("ens", None, "slab", None)
-    return jax.shard_map(shards, mesh=mesh, in_specs=in_specs, out_specs=out_specs, check_vma=False)
+
+    def run(ensemble, perturbation, ancestors, bathymetry):
+        body = functools.partial(cycle, mesh.shape["ens"]) if fits(mesh, ensemble) else shards
+        mapped = jax.shard_map(body, mesh=mesh, in_specs=in_specs, out_specs=out_specs, check_vma=False)
+        return mapped(ensemble, perturbation, ancestors, bathymetry)
+
+    return run

time: 423 us -> 40.5 us (0.10)
  other arithmetic: 226 us -> 0 us
  local copies, waits for them, and re-layouts: 130 us -> 1.92 us
  Pallas kernels: 0 us -> 37.7 us
  starting transfers between devices: 27.6 us -> 0 us
  waiting for transfers between devices: 22.3 us -> 0 us
  blocking collectives: 14.8 us -> 0 us
    unnamed x1 -> x0, other arithmetic: 219 us -> none
    unnamed x10 -> x1, local copies, waits for them, and re-layouts: 73 us -> 1.92 us
    pallas_call x0 -> x1, Pallas kernels: none -> 37.7 us  [cycle(): pl.pallas_call(functools.partial(cycle_kernel, n, rows, cols, across), ou...]
    another operation x4 -> x0, local copies, waits for them, and re-layouts: 36.1 us -> none  [shards(): flattened = jnp.stack(members).reshape(1, 3, row_count * col_count)]
    all_to_all x2 -> x0, waiting for transfers between devices: 19 us -> none  [the longest x1 19 us: shards(): lax.all_to_all(picked, 'ens', split_axis=0, concat_axis=2, tiled=True)]
    ppermute x8 -> x0, starting transfers between devices: 15.9 us -> none  [the longest x4 10.5 us: padded(): lax.ppermute(tail, axis, [(i, (i + 1) % count) for i in range(ends)])]
    unnamed x1 -> x0, blocking collectives: 14.8 us -> none
    all_to_all x2 -> x0, local copies, waits for them, and re-layouts: 14.3 us -> none  [the longest x1 14 us: shards(): lax.all_to_all(flattened, 'ens', split_axis=2, concat_axis=0, tiled=True)]
  transfers between devices with their start and end apart: 10 -> 0, of which waited for: 3 -> 0; matrix products, arithmetic and copies ran while one was open for 83% -> 0% of each run, Pallas kernels for 0% -> 0%
where the time goes in v1:
time: 40.5 us; the launch traced here: 40.3 us
  Pallas kernels  37.7 us (93%)
  local copies, waits for them, and re-layouts  1.92 us (5%)
  between operations  0.66 us (2%)
    pallas_call x1, Pallas kernels, cycle(): pl.pallas_call(functools.partial(cycle_kernel, n, rows, cols, across), ou...  37.7 us
    unnamed x1, local copies, waits for them, and re-layouts  1.92 us

profile of v1, /device:TPU:0, one launch (start us, length us, event | category | flops | bytes accessed | tf_op | source)
XLA Modules:
  0.0 40.3 jit_solution(16389663972164536907)
XLA Ops:
  0.7 37.7 %cycle.1 = f32[3,64,768]{2,1,0:T(8,128)} custom-call(f32[3,64,768]{2,1,0:T(8,128)} %bitcast.4, f32[3,64,768]{2,1,0:T(8,128)} %bitcast.5, s32[1]{0:T(128)S(6)} %copy.6.anc_ref, s32[128,768]{1,0:T(8,128)} %bath_ref.1), custom_call_target="tpu_custom_call" | custom-call | tf_op jit(solution)/shard_map/cycle/pallas_call | solution.py:308
  38.4 1.9 %copy.7 = f32[1,3,64,768]{3,2,1,0:T(8,128)} copy(f32[1,3,64,768]{3,2,1,0:T(8,128)} %bitcast.3) | data formatting | bytes 1179648

commit v2 on v1

--- a/solution.py
+++ b/solution.py
@@ -123,7 +123,7 @@
 def cycle_kernel(
     n, rows, cols, across,
     ens_ref, pert_ref, anc_ref, bath_ref, out_ref,
-    state, noise, sb, pieces0, pieces1, pieces2, picked, res, lin_v, lin_s,
+    state, noise, sb, seam, seam_sb, pieces0, pieces1, pieces2, picked, res, lin_v, lin_s,
     halo_send, halo_recv, lin_send, lin_recv, lin_local,
     a_send, a_recv, b_send, b_recv,
 ):
@@ -153,32 +153,67 @@
     pl.semaphore_signal(barrier, inc=1, device_id={"slab": 1 - s}, device_id_type=MESH)
 
     lin_v[me] = jnp.full((1, LANES), anc_ref[0], jnp.int32)
-    wall = pl.multiple_of(s * (rows + STRIP), STRIP)
-    open_side = pl.multiple_of((1 - s) * (rows + STRIP), STRIP)
     zeros = jnp.zeros((STRIP, cols), jnp.float32)
-    for f in range(3):
-        state[f, pl.ds(wall, STRIP)] = zeros
-        noise[f, pl.ds(wall, STRIP)] = zeros
-        for r in range(0, rows, STRIP):
+    first = pl.multiple_of(s * rows, STRIP)
+    for r in (0, bottom):
+        sb[r : r + STRIP] = zeros
+        for f in range(3):
+            state[f, r : r + STRIP] = zeros
+    for r in range(0, rows, STRIP):
+        depth = bath_ref[pl.ds(pl.multiple_of(first + r, STRIP), STRIP)]
+        sb[top + r : top + r + STRIP] = depth.astype(jnp.float32) * 0.01
+        for f in range(3):
             state[f, top + r : top + r + STRIP] = ens_ref[f, r : r + STRIP]
-            noise[f, top + r : top + r + STRIP] = pert_ref[f, r : r + STRIP]
-    sb[pl.ds(wall, STRIP)] = zeros
-    beyond = pl.multiple_of(rows - STRIP * s, STRIP)
-    sb[pl.ds(open_side, STRIP)] = bath_ref[pl.ds(beyond, STRIP)].astype(jnp.float32) * 0.01
-    first = pl.multiple_of(s * rows, STRIP)
-    for r in range(0, rows, STRIP):
-        sb[top + r : top + r + STRIP] = (
-            bath_ref[pl.ds(pl.multiple_of(first + r, STRIP), STRIP)].astype(jnp.float32) * 0.01
-        )
+    inner = pl.multiple_of((1 - s) * (rows - 2 * STRIP), STRIP)
+    for r in range(0, 3 * STRIP, STRIP):
+        depth = bath_ref[pl.ds(pl.multiple_of(rows - 2 * STRIP + s * STRIP + r, STRIP), STRIP)]
+        seam_sb[r : r + STRIP] = depth.astype(jnp.float32) * 0.01
+    for f in range(3):
+        for r in range(0, 2 * STRIP, STRIP):
+            seam[f, pl.ds(pl.multiple_of(s * STRIP + r, STRIP), STRIP)] = ens_ref[
+                f, pl.ds(pl.multiple_of(inner + r, STRIP), STRIP)
+            ]
+
+    def east(x):
+        return (pltpu.roll(x, cols - 1, 1) - pltpu.roll(x, 1, 1)) * 0.5
+
+    def shifted(ref, r, by):
+        if 0 <= r + by <= ref.shape[0] - STRIP:
+            return ref[r + by : r + by + STRIP]
+        return pltpu.roll(ref[r : r + STRIP], -by % STRIP, 0)
+
+    def heights(cells, floor, r):
+        here = slice(r, r + STRIP)
+        v = cells.at[2]
+        northward = shifted(floor, r, 1) * shifted(v, r, 1) - shifted(floor, r, -1) * shifted(v, r, -1)
+        eastward = east(floor[here] * cells[1, here])
+        cells[0, here] = cells[0, here] - RATIO * (eastward + northward * 0.5)
+
+    def velocities(cells, r):
+        here = slice(r, r + STRIP)
+        u = cells[1, here]
+        v = cells[2, here]
+        h = cells.at[0]
+        cells[1, here] = u - RATIO * east(h[here]) + TURNING * v
+        northward = (shifted(h, r, 1) - shifted(h, r, -1)) * 0.5
+        cells[2, here] = v - RATIO * northward - TURNING * u
+
+    for step in range(STEPS):
+        for r in range(top, bottom, STRIP):
+            heights(state, sb, r)
+        for r in range(top, bottom, STRIP):
+            velocities(state, r)
 
     pl.semaphore_wait(barrier, n)
 
     edge = pl.multiple_of((1 - s) * (rows - STRIP), STRIP)
     halos = []
-    for i, (src, dst) in enumerate(((ens_ref, state), (pert_ref, noise))):
+    for i, (src, dst, at) in enumerate(
+        ((ens_ref, seam, s * 2 * STRIP), (pert_ref, noise, s * (rows + STRIP)))
+    ):
         copy = pltpu.make_async_remote_copy(
             src_ref=src.at[:, pl.ds(edge, STRIP)],
-            dst_ref=dst.at[:, pl.ds(wall, STRIP)],
+            dst_ref=dst.at[:, pl.ds(pl.multiple_of(at, STRIP), STRIP)],
             send_sem=halo_send.at[i],
             recv_sem=halo_recv.at[i],
             device_id={"slab": 1 - s},
@@ -186,6 +221,34 @@
         )
         copy.start()
         halos.append(copy)
+
+    def spot(ref, f, index, base):
+        r = pl.multiple_of(base + (index // across) * STRIP, STRIP)
+        c = pl.multiple_of((index % across) * width, LANES)
+        return ref.at[f, pl.ds(r, STRIP), pl.ds(c, width)]
+
+    def deliver(f, to):
+        pltpu.make_async_remote_copy(
+            src_ref=spot(state, f, to, top),
+            dst_ref=pieces[f].at[me],
+            send_sem=a_send.at[f],
+            recv_sem=a_recv.at[f],
+            device_id={"ens": to},
+            device_id_type=MESH,
+        ).start()
+
+    def keep(f):
+        pltpu.make_async_copy(spot(state, f, me, top), pieces[f].at[me], a_recv.at[f]).start()
+
+    def at_seam(to):
+        return to // across == (1 - s) * (rows // STRIP - 1)
+
+    def early(t, to):
+        @pl.when(jnp.logical_not(at_seam(to)))
+        def _():
+            deliver(0, to)
+
+    each_peer(early)
 
     def tell(t, to):
         pltpu.make_async_remote_copy(
@@ -199,64 +262,31 @@
 
     each_peer(tell)
     halos[0].wait()
-
-    def shifted(f, r, by):
-        source = sb if f is None else state.at[f]
-        if 0 <= r + by <= rows + STRIP:
-            return source[r + by : r + by + STRIP]
-        return pltpu.roll(source[r : r + STRIP], -by % STRIP, 0)
-
-    def east(x):
-        return (pltpu.roll(x, cols - 1, 1) - pltpu.roll(x, 1, 1)) * 0.5
-
-    def heights(r):
-        here = slice(r, r + STRIP)
-        northward = shifted(None, r, 1) * shifted(2, r, 1) - shifted(None, r, -1) * shifted(2, r, -1)
-        new = state[0, here] - RATIO * (east(sb[here] * state[1, here]) + northward * 0.5)
-        if r == 0:
-            new = jnp.where(s == 1, new, 0.0)
-        if r == bottom:
-            new = jnp.where(s == 0, new, 0.0)
-        state[0, here] = new
-
-    def velocities(r):
-        here = slice(r, r + STRIP)
-        u = state[1, here]
-        v = state[2, here]
-        state[1, here] = u - RATIO * east(state[0, here]) + TURNING * v
-        northward = (shifted(0, r, 1) - shifted(0, r, -1)) * 0.5
-        state[2, here] = v - RATIO * northward - TURNING * u
-
-    def spot(ref, f, index, base):
-        r = pl.multiple_of(base + (index // across) * STRIP, STRIP)
-        c = pl.multiple_of((index % across) * width, LANES)
-        return ref.at[f, pl.ds(r, STRIP), pl.ds(c, width)]
-
-    def scatter(f):
-        def send(t, to):
-            pltpu.make_async_remote_copy(
-                src_ref=spot(state, f, to, top),
-                dst_ref=pieces[f].at[me],
-                send_sem=a_send.at[f],
-                recv_sem=a_recv.at[f],
-                device_id={"ens": to},
-                device_id_type=MESH,
-            ).start()
-
-        each_peer(send)
-        pltpu.make_async_copy(spot(state, f, me, top), pieces[f].at[me], a_recv.at[f]).start()
-
     for step in range(STEPS):
         last = step == STEPS - 1
-        for r in range(0, bottom + STRIP, STRIP):
-            heights(r)
-        if last:
-            scatter(0)
-        for r in range(top if last else 0, bottom if last else bottom + STRIP, STRIP):
-            velocities(r)
-    scatter(1)
-    scatter(2)
-
+        for r in range(0, 3 * STRIP, STRIP):
+            heights(seam, seam_sb, r)
+        for r in range(STRIP, 2 * STRIP, STRIP) if last else range(0, 3 * STRIP, STRIP):
+            velocities(seam, r)
+    for f in range(3):
+        state[f, pl.ds(pl.multiple_of(top + edge, STRIP), STRIP)] = seam[f, STRIP : 2 * STRIP]
+
+    def late(t, to):
+        @pl.when(at_seam(to))
+        def _():
+            deliver(0, to)
+
+    each_peer(late)
+    keep(0)
+    for f in (1, 2):
+        each_peer(lambda t, to, f=f: deliver(f, to))
+        keep(f)
+
+    wall = pl.multiple_of(s * (rows + STRIP), STRIP)
+    for f in range(3):
+        noise[f, pl.ds(wall, STRIP)] = zeros
+        for r in range(0, rows, STRIP):
+            noise[f, top + r : top + r + STRIP] = pert_ref[f, r : r + STRIP]
     halos[1].wait()
     for f in range(3):
         for r in range(top, bottom, STRIP):
@@ -314,6 +344,8 @@
             pltpu.VMEM((3, tall, cols), f32),
             pltpu.VMEM((3, tall, cols), f32),
             pltpu.VMEM((tall, cols), f32),
+            pltpu.VMEM((3, 3 * STRIP, cols), f32),
+            pltpu.VMEM((3 * STRIP, cols), f32),
             pltpu.VMEM((n, STRIP, cols // across), f32),
             pltpu.VMEM((n, STRIP, cols // across), f32),
             pltpu.VMEM((n, STRIP, cols // across), f32),

time: 40.5 us -> 38.2 us (0.943)
  Pallas kernels: 37.7 us -> 35.5 us
    pallas_call x1, Pallas kernels: 37.7 us -> 35.5 us  [cycle(): pl.pallas_call(functools.partial(cycle_kernel, n, rows, cols, across), ou...]
where the time goes in v2:
time: 38.2 us; the launch traced here: 38.1 us
  Pallas kernels  35.5 us (93%)
  local copies, waits for them, and re-layouts  1.92 us (5%)
  between operations  0.66 us (2%)
    pallas_call x1, Pallas kernels, cycle(): pl.pallas_call(functools.partial(cycle_kernel, n, rows, cols, across), ou...  35.5 us
    unnamed x1, local copies, waits for them, and re-layouts  1.92 us

profile of v2, /device:TPU:0, one launch (start us, length us, event | category | flops | bytes accessed | tf_op | source)
XLA Modules:
  0.0 38.1 jit_solution(14573195129118876714)
XLA Ops:
  0.7 35.5 %cycle.1 = f32[3,64,768]{2,1,0:T(8,128)} custom-call(f32[3,64,768]{2,1,0:T(8,128)} %bitcast.4, f32[3,64,768]{2,1,0:T(8,128)} %bitcast.5, s32[1]{0:T(128)S(6)} %copy.6.anc_ref, s32[128,768]{1,0:T(8,128)} %bath_ref.1), custom_call_target="tpu_custom_call" | custom-call | tf_op jit(solution)/shard_map/cycle/pallas_call | solution.py:338
  36.1 1.9 %copy.7 = f32[1,3,64,768]{3,2,1,0:T(8,128)} copy(f32[1,3,64,768]{3,2,1,0:T(8,128)} %bitcast.3) | data formatting | bytes 1179648

commit v3 on v2

--- a/solution.py
+++ b/solution.py
@@ -123,8 +123,8 @@
 def cycle_kernel(
     n, rows, cols, across,
     ens_ref, pert_ref, anc_ref, bath_ref, out_ref,
-    state, noise, sb, seam, seam_sb, pieces0, pieces1, pieces2, picked, res, lin_v, lin_s,
-    halo_send, halo_recv, lin_send, lin_recv, lin_local,
+    state, noise, sb, seam, seam_sb, bath_v, pieces0, pieces1, pieces2, picked, res, lin_v, lin_s,
+    halo_send, halo_recv, lin_send, lin_recv, lin_local, loads,
     a_send, a_recv, b_send, b_recv,
 ):
     me = lax.axis_index("ens")
@@ -153,26 +153,38 @@
     pl.semaphore_signal(barrier, inc=1, device_id={"slab": 1 - s}, device_id_type=MESH)
 
     lin_v[me] = jnp.full((1, LANES), anc_ref[0], jnp.int32)
+    inner = pl.multiple_of((1 - s) * (rows - 2 * STRIP), STRIP)
+    fills = [
+        pltpu.make_async_copy(src, dst, loads.at[i])
+        for i, (src, dst) in enumerate(
+            (
+                (bath_ref, bath_v),
+                (ens_ref, state.at[:, pl.ds(top, rows)]),
+                (
+                    ens_ref.at[:, pl.ds(inner, 2 * STRIP)],
+                    seam.at[:, pl.ds(pl.multiple_of(s * STRIP, STRIP), 2 * STRIP)],
+                ),
+                (pert_ref, noise.at[:, pl.ds(top, rows)]),
+            )
+        )
+    ]
+    for fill in fills:
+        fill.start()
     zeros = jnp.zeros((STRIP, cols), jnp.float32)
     first = pl.multiple_of(s * rows, STRIP)
     for r in (0, bottom):
         sb[r : r + STRIP] = zeros
         for f in range(3):
             state[f, r : r + STRIP] = zeros
+    fills[0].wait()
     for r in range(0, rows, STRIP):
-        depth = bath_ref[pl.ds(pl.multiple_of(first + r, STRIP), STRIP)]
+        depth = bath_v[pl.ds(pl.multiple_of(first + r, STRIP), STRIP)]
         sb[top + r : top + r + STRIP] = depth.astype(jnp.float32) * 0.01
-        for f in range(3):
-            state[f, top + r : top + r + STRIP] = ens_ref[f, r : r + STRIP]
-    inner = pl.multiple_of((1 - s) * (rows - 2 * STRIP), STRIP)
     for r in range(0, 3 * STRIP, STRIP):
-        depth = bath_ref[pl.ds(pl.multiple_of(rows - 2 * STRIP + s * STRIP + r, STRIP), STRIP)]
+        depth = bath_v[pl.ds(pl.multiple_of(rows - 2 * STRIP + s * STRIP + r, STRIP), STRIP)]
         seam_sb[r : r + STRIP] = depth.astype(jnp.float32) * 0.01
-    for f in range(3):
-        for r in range(0, 2 * STRIP, STRIP):
-            seam[f, pl.ds(pl.multiple_of(s * STRIP + r, STRIP), STRIP)] = ens_ref[
-                f, pl.ds(pl.multiple_of(inner + r, STRIP), STRIP)
-            ]
+    fills[1].wait()
+    fills[2].wait()
 
     def east(x):
         return (pltpu.roll(x, cols - 1, 1) - pltpu.roll(x, 1, 1)) * 0.5
@@ -285,8 +297,7 @@
     wall = pl.multiple_of(s * (rows + STRIP), STRIP)
     for f in range(3):
         noise[f, pl.ds(wall, STRIP)] = zeros
-        for r in range(0, rows, STRIP):
-            noise[f, top + r : top + r + STRIP] = pert_ref[f, r : r + STRIP]
+    fills[3].wait()
     halos[1].wait()
     for f in range(3):
         for r in range(top, bottom, STRIP):
@@ -334,11 +345,16 @@
     tall = rows + 2 * STRIP
     f32 = jnp.float32
     vmem = pl.BlockSpec(memory_space=pltpu.VMEM)
+    hbm = pl.BlockSpec(memory_space=pltpu.HBM)
     dma = pltpu.SemaphoreType.DMA
+    held = [
+        pltpu.with_memory_space_constraint(x, pltpu.HBM)
+        for x in (ensemble[0], perturbation[0], bathymetry)
+    ]
     result = pl.pallas_call(
         functools.partial(cycle_kernel, n, rows, cols, across),
         out_shape=jax.ShapeDtypeStruct((3, rows, cols), f32),
-        in_specs=[vmem, vmem, pl.BlockSpec(memory_space=pltpu.SMEM), vmem],
+        in_specs=[hbm, hbm, pl.BlockSpec(memory_space=pltpu.SMEM), hbm],
         out_specs=vmem,
         scratch_shapes=[
             pltpu.VMEM((3, tall, cols), f32),
@@ -346,6 +362,7 @@
             pltpu.VMEM((tall, cols), f32),
             pltpu.VMEM((3, 3 * STRIP, cols), f32),
             pltpu.VMEM((3 * STRIP, cols), f32),
+            pltpu.VMEM(bathymetry.shape, jnp.int32),
             pltpu.VMEM((n, STRIP, cols // across), f32),
             pltpu.VMEM((n, STRIP, cols // across), f32),
             pltpu.VMEM((n, STRIP, cols // across), f32),
@@ -353,12 +370,12 @@
             pltpu.VMEM((3, rows, cols), f32),
             pltpu.VMEM((n, 1, LANES), jnp.int32),
             pltpu.SMEM((n, 1, LANES), jnp.int32),
-            dma((2,)), dma((2,)), dma(()), dma(()), dma(()),
+            dma((2,)), dma((2,)), dma(()), dma(()), dma(()), dma((4,)),
             dma((3,)), dma((3,)), dma((3,)), dma((3,)),
         ],
-        compiler_params=pltpu.CompilerParams(collective_id=0, has_side_effects=True),
+        compiler_params=pltpu.CompilerParams(collective_id=0, has_side_effects=True, vmem_limit_bytes=24 << 20),
         name="cycle",
-    )(ensemble[0], perturbation[0], ancestors, bathymetry)
+    )(*held[:2], ancestors, held[2])
     return result[None]
 
 

time: 38.2 us -> 36.2 us (0.948)
  local copies, waits for them, and re-layouts: 1.92 us -> 0.82 us
  Pallas kernels: 35.5 us -> 34.6 us
    unnamed x1, local copies, waits for them, and re-layouts: 1.92 us -> 0.82 us
    pallas_call x1, Pallas kernels: 35.5 us -> 34.6 us  [cycle(): pl.pallas_call(functools.partial(cycle_kernel, n, rows, cols, across), ou...]
where the time goes in v3:
time: 36.2 us; the launch traced here: 36 us
  Pallas kernels  34.6 us (96%)
  local copies, waits for them, and re-layouts  0.82 us (2%)
  between operations  0.66 us (2%)
    pallas_call x1, Pallas kernels, cycle(): pl.pallas_call(functools.partial(cycle_kernel, n, rows, cols, across), ou...  34.6 us
    unnamed x1, local copies, waits for them, and re-layouts  0.82 us

profile of v3, /device:TPU:0, one launch (start us, length us, event | category | flops | bytes accessed | tf_op | source)
XLA Modules:
  0.0 36.0 jit_solution(17193858557065859416)
XLA Ops:
  0.7 34.6 %cycle.1 = f32[3,64,768]{2,1,0:T(8,128)S(1)} custom-call(f32[3,64,768]{2,1,0:T(8,128)} %bitcast.4, f32[3,64,768]{2,1,0:T(8,128)} %bitcast.5, s32[1]{0:T(128)S(6)} %copy.6.anc_ref, s32[128,768]{1,0:T(8,128)} %bath_ref.1), custom_call_target="tpu_custom_call" | custom-call | tf_op jit(solution)/shard_map/cycle/pallas_call | solution.py:354
  35.2 0.8 %copy.7 = f32[1,3,64,768]{3,2,1,0:T(8,128)} copy(f32[1,3,64,768]{3,2,1,0:T(8,128)S(1)} %bitcast.3) | data formatting | bytes 1179648
